TPU v7x, 256 devices: a whole 4x4x8 slice. The times are simulated.
256 devices in a mesh: dp: 8 (over x, core), vocab: 16 (over z_hi, y), width: 2 (over z_lo).
Axes of the slice: x: 4, y: 4, z: 8 (z_hi: 4, z_lo: 2; z = z_hi * 2 + z_lo), core: 2. Of those that a mesh axis runs over, the one named last changes fastest.
Arguments:
- hidden: bfloat16 [8192, 5376], P(('dp', 'vocab'), 'width'), may hold values from -1000 to 1000, as said below
- rest_lse: bfloat16 [8192], P(('dp', 'vocab')), may hold values from 0 to 800
- token_ids: int32 [8192], P(('dp', 'vocab')), may hold values from 0 to 32767
- slab_offset: int32 [1], replicated, may hold values from 0 to 16384
- embedding: bfloat16 [16384, 5376], P('vocab', 'width'), may hold values from -0.078125 to 0.078125
- row_state: float32 [16384], P(('vocab', 'dp')), may hold values from 0.001 to 5, as said below
- col_state: float32 [5376], P('width'), may hold values from 0.003 to 0.3
Outputs:
- update: float32 [16384, 5376], P(('vocab', 'dp'), 'width')
- new_rows: float32 [16384], P(('vocab', 'dp'))
- new_cols: float32 [5376], P('width')
- row_mean: float32 [1], replicated
Inputs may be any that keep to these rules, and one draw needn't show every extreme that they name: `hidden`: entries stay within the stated range. `row_state`: entries are positive.
All inputs are finite; a program needn't handle non-finite values.
Results may differ from a plain program's by a relative error of at most 0.0012.
Values may be sent and summed in bfloat16 or wider, within the bound.
A program may use at most 64 MiB of HBM per device.

v0:
```python
import functools
import math

import jax
import jax.numpy as jnp
from jax import lax
from jax.sharding import Mesh
from jax.sharding import PartitionSpec as P

VOCAB = ("vocab_0", "vocab_1")
DP = ("dp_0", "dp_1")
DP_VOCAB = ("dp_0", "dp_1", "vocab_0", "vocab_1")
DP_VOCAB_WIDTH = ("dp_0", "dp_1", "vocab_0", "vocab_1", "width")
VOCAB_DP = ("vocab_0", "vocab_1", "dp_0", "dp_1")


def sent_to_all(shard, axis):
    peers = lax.axis_size(axis)
    return lax.all_to_all(
        jnp.broadcast_to(shard[None], (peers, *shard.shape)), axis, 0, 0, tiled=True
    )


def gathered_once(shard, axis):
    leaves = jax.tree.leaves(shard)
    sequence = sorted(range(len(leaves)), key=lambda k: -leaves[k].size)
    width = (1, *leaves[sequence[0]].shape)[-1]
    lines = [
        jnp.pad(leaves[k].reshape(-1), (0, -leaves[k].size % width)).reshape(-1, width)
        for k in sequence
    ]
    both, at, found = (sent_to_all(jnp.concatenate(lines), axis), 0, {})
    for k, line in zip(sequence, lines):
        share = both[:, at : at + len(line)].reshape(len(both), -1)
        found[k] = share[:, : leaves[k].size].reshape(-1, *leaves[k].shape)
        at += len(line)
    numbers = iter(range(len(leaves)))
    return jax.tree.map(lambda _: found[next(numbers)], shard)


def combined_pairwise(pieces, combine):
    while len(jax.tree.leaves(pieces)[0]) > 1:
        pieces = jax.vmap(combine)(
            *(jax.tree.map(lambda part: part[side::2], pieces) for side in (0, 1))
        )
    return jax.tree.map(lambda part: part[0], pieces)


def combined_all(shard, axis, combine):
    pieces = gathered_once(shard, axis)
    return combined_pairwise(pieces, combine)


def in_one_piece(arrays, axis, dim, along):
    widths = [math.prod(a.shape[along:]) for a in arrays]
    both = jnp.concatenate(
        [a.reshape(*a.shape[:along], w) for a, w in zip(arrays, widths)], axis=along
    )
    whole = lax.all_gather(both, axis, axis=dim, tiled=True)
    blocks = jnp.split(whole, [sum(widths[:k]) for k in range(1, len(widths))], axis=along)
    return tuple(
        (b.reshape(*whole.shape[:along], *a.shape[along:]) for a, b in zip(arrays, blocks))
    )


def joined_along(blocks, dim):
    shape = list(blocks.shape[1:])
    shape[dim] *= blocks.shape[0]
    return jnp.moveaxis(blocks, 0, dim).reshape(shape)


def gather_directly(shard, axis, dim):
    return joined_along(sent_to_all(shard, axis), dim)


def split_up(shard, dim, peers):
    before, after = (shard.shape[:dim], shard.shape[dim + 1 :])
    return jnp.moveaxis(shard.reshape(*before, peers, -1, *after), dim, 0)


def sent_and_summed(shard, axis, dim):
    peers = lax.axis_size(axis)
    blocks = lax.all_to_all(split_up(shard, dim, peers), axis, 0, 0, tiled=True)
    return jnp.sum(blocks, axis=0)


def of_everyone(shard, axis):
    return sent_to_all(shard, axis).sum(axis=0)


def by_axis(shard, axes):
    return functools.reduce(lax.psum, axes, shard)


def combine_stats(first, second):
    peak = jnp.maximum(first[0], second[0])
    return (peak, first[1] * jnp.exp(first[0] - peak) + second[1] * jnp.exp(second[0] - peak))


def logit_grads(logits, rest, labels, offset, base):
    top = jnp.max(logits, axis=1)
    total = jnp.sum(jnp.exp(logits - top[:, None]), axis=1)
    top, total = combined_all((top, total), VOCAB, combine_stats)
    rest_value = rest.astype(jnp.float32)
    big = jnp.maximum(top, rest_value)
    lse = big + jnp.log(total * jnp.exp(top - big) + jnp.exp(rest_value - big))
    row_index = base + jnp.arange(logits.shape[1], dtype=jnp.int32)
    hit = labels[:, None] - offset == row_index[None, :]
    return (jnp.exp(logits - lse[:, None]) - hit.astype(jnp.float32)).astype(jnp.bfloat16)


def per_device(hidden, rest_lse, token_ids, slab_offset, embedding, row_state, col_state):
    states, rest = in_one_piece((hidden, rest_lse), VOCAB, 0, 1)
    labels = gather_directly(token_ids, VOCAB, 0)
    block_rows = embedding.shape[0]
    base = lax.axis_index(VOCAB) * block_rows
    offset = slab_offset[0]
    partial_logits = lax.dot_general(
        states, embedding, (((1,), (1,)), ((), ())), preferred_element_type=jnp.float32
    )
    share = sent_and_summed(partial_logits, "width", 0)
    count = share.shape[0]
    start = lax.axis_index("width") * count
    rest_part = lax.dynamic_slice_in_dim(rest, start, count)
    label_part = lax.dynamic_slice_in_dim(labels, start, count)
    dlogits = gather_directly(logit_grads(share, rest_part, label_part, offset, base), "width", 0)
    full_grad = lax.dot_general(
        dlogits, states, (((0,), (0,)), ((), ())), preferred_element_type=jnp.float32
    )
    grad = lax.psum_scatter(full_grad, DP, scatter_dimension=0, tiled=True)
    slab_rows = block_rows * lax.axis_size(VOCAB)
    full_width = grad.shape[1] * lax.axis_size("width")
    square = grad * grad + 1e-06
    row_part = jnp.sum(square, axis=1)
    col_part = jnp.sum(square, axis=0)
    row_sq = of_everyone(row_part, "width")
    col_sq = by_axis(col_part, DP_VOCAB)
    new_rows = 0.9 * row_state + 0.1 * row_sq / full_width
    rows_total = by_axis(jnp.sum(new_rows), DP_VOCAB)
    new_cols = 0.9 * col_state + 0.1 * col_sq / slab_rows
    mean_rows = rows_total / slab_rows
    raw = grad * lax.rsqrt(new_rows[:, None] * new_cols[None, :] / mean_rows)
    square_total = by_axis(jnp.sum(raw * raw), DP_VOCAB_WIDTH)
    rms = jnp.sqrt(square_total / (slab_rows * full_width))
    update = raw / jnp.maximum(1.0, rms / 0.1)
    return (update, new_rows, new_cols, jnp.reshape(mean_rows, (1,)))


def solution(mesh):
    finer = Mesh(
        mesh.devices.reshape(4, 2, 4, 4, mesh.shape["width"]),
        ("dp_0", "dp_1", "vocab_0", "vocab_1", "width"),
    )
    placed = (
        P(DP_VOCAB, "width"),
        P(DP_VOCAB),
        P(DP_VOCAB),
        P(),
        P(VOCAB, "width"),
        P(VOCAB_DP),
        P("width"),
    )
    return jax.shard_map(
        per_device,
        mesh=finer,
        in_specs=placed,
        out_specs=(P(VOCAB_DP, "width"), P(VOCAB_DP), P("width"), P()),
        check_vma=False,
    )
```

profile of v0, /device:TPU:10, one launch (start us, length us, event | category | flops | bytes accessed | tf_op | source)
XLA Modules:
  0.0 407.8 jit_solution(14816101541274686650)
XLA Ops:
  7.2 0.8 copy.20
  8.0 1.7 pad_maximum_fusion
  9.7 1.3 broadcast_in_dim.9
  11.0 11.6 %all-to-all-start.2 = ((s32[16,1,64]{2,1,0:T(1,128)}), s32[16,1,64]{2,1,0:T(1,128)S(1)}, u32[]{:S(2)}, u32[]{:S(2)}) async-start(s32[16,1,64]{2,1,0:T(1,128)} %broadcast_in_dim.9), calls=%async_computation.2 | async-start | bytes 16384 | tf_op jit(solution)/shard_map/all_to_all | solution.py:19
  22.6 75.4 %all-gather.2.cloned.1.call-done = bf16[1024,2689]{1,0:T(8,128)(2,1)} async-done(((bf16[64,2689]{1,0:T(8,128)(2,1)}), bf16[1024,2689]{1,0:T(8,128)(2,1)}) %all-gather.2.cloned.1.call-update) | async-done | bytes 5507088 | tf_op jit(solution)/shard_map/all_gather | solution.py:59
  97.9 11.1 %fusion.2 = f32[1024,1024]{1,0:T(8,128)} fusion(bf16[1024,2688]{1,0:T(8,128)(2,1)} %param.11, bf16[1024,2689]{1,0:T(8,128)(2,1)} %all-gather.2.cloned.1.call-done), kind=kOutput, calls=%fused_computation.2 | convolution fusion | flops 5637144576 | bytes 15204352 | tf_op jit(solution)/shard_map/dot_general | solution.py:118
  109.1 10.3 %all-to-all-start = ((f32[2,512,1024]{2,1,0:T(8,128)}), f32[2,512,1024]{2,1,0:T(8,128)}, u32[]{:S(2)}, u32[]{:S(2)}) async-start(f32[2,512,1024]{2,1,0:T(8,128)} %bitcast.39), calls=%async_computation | async-start | bytes 8388608 | tf_op jit(solution)/shard_map/all_to_all | solution.py:83
  120.0 0.5 broadcast.46
  120.5 0.7 reduce.4
  121.3 48.5 %all-to-all-done = f32[2,512,1024]{2,1,0:T(8,128)} async-done(((f32[2,512,1024]{2,1,0:T(8,128)}), f32[2,512,1024]{2,1,0:T(8,128)}, u32[]{:S(2)}, u32[]{:S(2)}) %all-to-all-start) | async-done | bytes 4194336 | tf_op jit(solution)/shard_map/all_to_all | solution.py:83
  169.8 2.8 reduce_sum.63
  173.2 0.7 broadcast_in_dim.8
  173.9 7.0 %all-to-all-start.1 = ((f32[16,2,512]{2,1,0:T(2,128)}), f32[16,2,512]{2,1,0:T(2,128)S(1)}, u32[]{:S(2)}, u32[]{:S(2)}) async-start(f32[16,2,512]{2,1,0:T(2,128)} %broadcast_in_dim.8), calls=%async_computation.1 | async-start | bytes 131072 | tf_op jit(solution)/shard_map/all_to_all | solution.py:19
  181.1 8.5 %all-to-all-done.1 = f32[16,2,512]{2,1,0:T(2,128)S(1)} async-done(((f32[16,2,512]{2,1,0:T(2,128)}), f32[16,2,512]{2,1,0:T(2,128)S(1)}, u32[]{:S(2)}, u32[]{:S(2)}) %all-to-all-start.1) | async-done | bytes 65568 | tf_op jit(solution)/shard_map/all_to_all | solution.py:19
  190.0 0.5 subtract_convert_fusion
  190.9 25.6 %all_to_all.27 = bf16[2,512,1024]{2,1,0:T(8,128)(2,1)S(1)} all-to-all(bf16[2,512,1024]{2,1,0:T(8,128)(2,1)S(1)} %broadcast_in_dim.10), channel_id=1, replica_groups=mesh['dp_0'=4,'dp_1'=2,'vocab_0'=4,'vocab_1'=4,'width'=2] {'width'}, dimensions={0} | all-to-all | bytes 4194304 | tf_op jit(solution)/shard_map/all_to_all | solution.py:19
  216.5 11.5 %fusion = f32[1024,2688]{1,0:T(8,128)} fusion(bf16[1024,1024]{1,0:T(8,128)(2,1)S(1)} %bitcast.40, bf16[1024,2689]{1,0:T(8,128)(2,1)} %all-gather.2.cloned.1.call-done), kind=kOutput, calls=%fused_computation | convolution fusion | flops 5637144576 | bytes 18612224 | tf_op jit(solution)/shard_map/dot_general | solution.py:127
  228.0 61.3 %reduce-scatter.2.cloned.1.call-done = f32[128,2688]{1,0:T(8,128)} async-done(((f32[1024,2688]{1,0:T(8,128)}), f32[128,2688]{1,0:T(8,128)}) %reduce-scatter.2.cloned.1.call-update) | async-done | bytes 1376272 | tf_op jit(solution)/shard_map/reduce_scatter | solution.py:130
  289.3 1.7 fusion.4
  291.0 6.4 %all_to_all.28 = f32[2,1,128]{2,1,0:T(1,128)S(1)} all-to-all(f32[2,1,128]{2,1,0:T(1,128)S(1)} %broadcast_in_dim.11), channel_id=1, replica_groups=mesh['dp_0'=4,'dp_1'=2,'vocab_0'=4,'vocab_1'=4,'width'=2] {'width'}, dimensions={0} | all-to-all | bytes 2048 | tf_op jit(solution)/shard_map/all_to_all | solution.py:19
  297.4 0.6 fusion.14
  298.0 16.1 %all-reduce.2 = (f32[]{:T(128)}, f32[2688]{0:T(1024)S(1)}) all-reduce(f32[]{:T(128)} %get-tuple-element.14, f32[2688]{0:T(1024)S(1)} %get-tuple-element.4), channel_id=1, replica_groups=mesh['dp_0'=4,'dp_1'=2,'vocab_0'=4,'vocab_1'=4,'width'=2] {'dp_0'}, use_global_device_ids=true, to_apply=%region_12.13 | all-reduce | flops 2689 | bytes 21512 | tf_op jit(solution)/shard_map/psum | solution.py:92
  314.1 4.4 %all-reduce.3 = (f32[]{:T(128)}, f32[2688]{0:T(1024)S(1)}) all-reduce(f32[]{:T(128)} %get-tuple-element.10, f32[2688]{0:T(1024)S(1)} %get-tuple-element.11), channel_id=1, replica_groups=mesh['dp_0'=4,'dp_1'=2,'vocab_0'=4,'vocab_1'=4,'width'=2] {'dp_1'}, use_global_device_ids=true, to_apply=%region_13.14 | all-reduce | flops 2689 | bytes 21512 | tf_op jit(solution)/shard_map/psum | solution.py:92
  318.5 20.9 %all-reduce.1 = (f32[]{:T(128)}, f32[2688]{0:T(1024)S(1)}) all-reduce(f32[]{:T(128)} %get-tuple-element.12, f32[2688]{0:T(1024)S(1)} %get-tuple-element.13), channel_id=1, replica_groups=mesh['dp_0'=4,'dp_1'=2,'vocab_0'=4,'vocab_1'=4,'width'=2] {'vocab_0'}, use_global_device_ids=true, to_apply=%region_14.15 | all-reduce | flops 2689 | bytes 21512 | tf_op jit(solution)/shard_map/psum | solution.py:92
  339.4 15.0 %all-reduce = (f32[]{:T(128)}, f32[2688]{0:T(1024)S(1)}) all-reduce(f32[]{:T(128)} %get-tuple-element.8, f32[2688]{0:T(1024)S(1)} %get-tuple-element.9), channel_id=1, replica_groups=mesh['dp_0'=4,'dp_1'=2,'vocab_0'=4,'vocab_1'=4,'width'=2] {'vocab_1'}, use_global_device_ids=true, to_apply=%region_15.16 | all-reduce | flops 2689 | bytes 21512 | tf_op jit(solution)/shard_map/psum | solution.py:92
  355.1 1.0 multiply_reduce_fusion
  356.2 11.0 %psum.99 = f32[]{:T(128)} all-reduce(f32[]{:T(128)} %multiply_reduce_fusion), channel_id=1, replica_groups=mesh['dp_0'=4,'dp_1'=2,'vocab_0'=4,'vocab_1'=4,'width'=2] {'dp_0'}, use_global_device_ids=true, to_apply=%region_17.18 | all-reduce | flops 1 | bytes 8 | tf_op jit(solution)/shard_map/psum | solution.py:92
  367.2 3.1 psum.100
  370.2 10.2 %psum.101 = f32[]{:T(128)} all-reduce(f32[]{:T(128)} %psum.100), channel_id=1, replica_groups=mesh['dp_0'=4,'dp_1'=2,'vocab_0'=4,'vocab_1'=4,'width'=2] {'vocab_0'}, use_global_device_ids=true, to_apply=%region_19.20 | all-reduce | flops 1 | bytes 8 | tf_op jit(solution)/shard_map/psum | solution.py:92
  380.4 11.8 %psum.102 = f32[]{:T(128)} all-reduce(f32[]{:T(128)} %psum.101), channel_id=1, replica_groups=mesh['dp_0'=4,'dp_1'=2,'vocab_0'=4,'vocab_1'=4,'width'=2] {'vocab_1'}, use_global_device_ids=true, to_apply=%region_20.21 | all-reduce | flops 1 | bytes 8 | tf_op jit(solution)/shard_map/psum | solution.py:92
  392.3 5.5 %psum.103 = f32[]{:T(128)} all-reduce(f32[]{:T(128)} %psum.102), channel_id=1, replica_groups=mesh['dp_0'=4,'dp_1'=2,'vocab_0'=4,'vocab_1'=4,'width'=2] {'width'}, use_global_device_ids=true, to_apply=%region_21.22 | all-reduce | flops 1 | bytes 8 | tf_op jit(solution)/shard_map/psum | solution.py:92
  398.5 1.4 broadcast_divide_fusion
  (47 shorter events, 1.8 us)
Async XLA Ops:
  7.2 90.8 %all-gather.2.cloned.1.call-start = ((), (), s32[]{:S(2)}) async-start(), calls=%async_computation.6 | async-start | bytes 6127616 | tf_op jit(solution)/shard_map/all_gather | solution.py:59
  11.0 98.1 %all-to-all-start.2 = ((s32[16,1,64]{2,1,0:T(1,128)}), s32[16,1,64]{2,1,0:T(1,128)S(1)}, u32[]{:S(2)}, u32[]{:S(2)}) async-start(s32[16,1,64]{2,1,0:T(1,128)} %broadcast_in_dim.9), calls=%async_computation.2 | async-start | bytes 16384 | tf_op jit(solution)/shard_map/all_to_all | solution.py:19
  109.1 60.7 %all-to-all-start = ((f32[2,512,1024]{2,1,0:T(8,128)}), f32[2,512,1024]{2,1,0:T(8,128)}, u32[]{:S(2)}, u32[]{:S(2)}) async-start(f32[2,512,1024]{2,1,0:T(8,128)} %bitcast.39), calls=%async_computation | async-start | bytes 8388608 | tf_op jit(solution)/shard_map/all_to_all | solution.py:83
  172.6 8.4 %slice-start = ((bf16[1024,2689]{1,0:T(8,128)(2,1)}), bf16[1024,1]{1,0:T(8,128)(2,1)S(1)}, s32[]{:S(2)}) async-start(bf16[1024,2689]{1,0:T(8,128)(2,1)} %all-gather.2.cloned.1.call-done), calls=%async_computation.8 | async-start | bytes 524288 | tf_op jit(solution)/shard_map/split | solution.py:60
  173.9 15.7 %all-to-all-start.1 = ((f32[16,2,512]{2,1,0:T(2,128)}), f32[16,2,512]{2,1,0:T(2,128)S(1)}, u32[]{:S(2)}, u32[]{:S(2)}) async-start(f32[16,2,512]{2,1,0:T(2,128)} %broadcast_in_dim.8), calls=%async_computation.1 | async-start | bytes 131072 | tf_op jit(solution)/shard_map/all_to_all | solution.py:19
  180.9 108.4 %reduce-scatter.2.cloned.1.call-start = ((), (), s32[]{:S(2)}) async-start(), calls=%async_computation.7 | async-start | bytes 12386304 | tf_op jit(solution)/shard_map/reduce_scatter | solution.py:130
  227.9 69.5 %copy-start.4 = (f32[128]{0:T(128)S(1)}, f32[128]{0:T(128)}, u32[]{:S(2)}) copy-start(f32[128]{0:T(128)} %param.12) | copy-start | bytes 1540
  227.9 127.1 %copy-start.2 = (f32[2688]{0:T(1024)S(1)}, f32[2688]{0:T(1024)}, u32[]{:S(2)}) copy-start(f32[2688]{0:T(1024)} %param.13) | copy-start | bytes 32260
  289.3 65.9 %copy-start = (f32[128,2688]{1,0:T(8,128)S(1)}, f32[128,2688]{1,0:T(8,128)}, u32[]{:S(2)}) copy-start(f32[128,2688]{1,0:T(8,128)} %reduce-scatter.2.cloned.1.call-done) | copy-start | bytes 4128772
  298.0 101.9 %copy-start.3 = (f32[128]{0:T(128)}, f32[128]{0:T(128)S(1)}, u32[]{:S(2)}) copy-start(f32[128]{0:T(128)S(1)} %get-tuple-element.15) | copy-start | bytes 1540
  355.1 44.8 %copy-start.1 = (f32[2688]{0:T(1024)}, f32[2688]{0:T(1024)S(1)}, u32[]{:S(2)}) copy-start(f32[2688]{0:T(1024)S(1)} %multiply_add_fusion.2) | copy-start | bytes 32260
Sparse Core Ops, SparseCore 0:
  11.0 86.9 all-gather.1
  228.1 61.1 reduce-scatter.1
where the time goes:
time: 409 us; the launch traced here: 408 us
  waiting for transfers between devices  194 us (47%)
  blocking collectives  130 us (32%)
  starting transfers between devices  28.9 us (7%)
  matrix products  22.6 us (6%)
  between operations  17.3 us (4%)
  other arithmetic  11.3 us (3%)
    psum x9, blocking collectives, by_axis(): return functools.reduce(lax.psum, axes, shard)  98.1 us
    all_gather x1, waiting for transfers between devices, in_one_piece(): whole = lax.all_gather(both, axis, axis=dim, tiled=True)  75.4 us
    reduce_scatter x1, waiting for transfers between devices, per_device(): grad = lax.psum_scatter(full_grad, DP, scatter_dimension=0, tiled=True)  61.3 us
    all_to_all x1, waiting for transfers between devices, sent_and_summed(): blocks = lax.all_to_all(split_up(shard, dim, peers), axis, 0, 0, tiled=True)  48.5 us
    all_to_all x2, blocking collectives, sent_to_all(): lax.all_to_all(jnp.broadcast_to(shard[None], (peers, *shard.shape)), axis...  32 us
    all_to_all x2, starting transfers between devices, sent_to_all(): lax.all_to_all(jnp.broadcast_to(shard[None], (peers, *shard.shape)), axis...  18.5 us
    dot_general x1, matrix products, per_device(): lax.dot_general(dlogits, states, (((0,), (0,)), ((), ())), preferred_elem...  11.5 us
    dot_general x1, matrix products, per_device(): lax.dot_general(states, embedding, (((1,), (1,)), ((), ())), preferred_el...  11.1 us
  transfers between devices with their start and end apart: 5, of which 4 were waited for; matrix products, arithmetic and copies ran while one was open for 3% of the time, Pallas kernels for 0%

commit v1 on v0

v1 whole, which is shorter than its diff:
```python
import functools

import jax
import jax.numpy as jnp
from jax import lax
from jax.experimental import pallas as pl
from jax.experimental.pallas import tpu as pltpu
from jax.sharding import Mesh
from jax.sharding import PartitionSpec as P

VOCAB = ("vocab_0", "vocab_1")
DP_VOCAB = ("dp_0", "dp_1", "vocab_0", "vocab_1")
VOCAB_DP = ("vocab_0", "vocab_1", "dp_0", "dp_1")
MESH = pl.DeviceIdType.MESH
F32 = jnp.float32
BF16 = jnp.bfloat16

SHARD = 64
CHUNK = 256
HALF = 128
ROWS = 1024
BLK = 128
K = 2688
TILES = K // 128
SLAB = 16384
FULL = 5376
TOKENS_TOTAL_TILES = 43
PER = 6
NW = 896
NP = K // NW


def kernel(hid, aux, emb, row_state, col_state,
           upd, nrows_out, ncols_out, mean_out,
           h0, h1, ev, ar, lown, lsend, lrecv, st, sr, lse,
           da, db, rpair, rsib, rdiag, part, ra, rb, fa, fb,
           rowp, rowx, vec, vr, ss, s2r, wv, qv, qx,
           local_sem, aux_s, aux_r, z_s, z_r, y_s, y_r, sib_s, sib_r, l_s, l_r,
           st_s, st_r, d_s, d_r, rs_s, rs_r, row_sem, v_s, v_r, s2_s, s2_r, w_s, w_r, q_sem):
    x = lax.axis_index("dp_0")
    c = lax.axis_index("dp_1")
    zh = lax.axis_index("vocab_0")
    y = lax.axis_index("vocab_1")
    w = lax.axis_index("width")
    d = x * 2 + c
    v = zh * 4 + y

    def plus(a, b):
        return lax.rem(a + b, 4)

    voc = [(oz, oy) for oz in range(4) for oy in range(4) if (oz, oy) != (0, 0)]
    dps = [(ox, oc) for ox in range(4) for oc in range(2) if (ox, oc) != (0, 0)]

    def to_voc(oz, oy):
        return {"vocab_0": plus(zh, oz), "vocab_1": plus(y, oy)}

    def to_dp(ox, oc):
        return {"dp_0": plus(x, ox), "dp_1": lax.rem(c + oc, 2)}

    pair = {"width": 1 - w}
    sib = {"dp_1": 1 - c}
    diag = {"width": 1 - w, "dp_1": 1 - c}
    zp, zm = {"vocab_0": plus(zh, 1)}, {"vocab_0": plus(zh, 3)}
    yp, ym = {"vocab_1": plus(y, 1)}, {"vocab_1": plus(y, 3)}
    xp, xm = {"dp_0": plus(x, 1)}, {"dp_0": plus(x, 3)}

    barrier = pltpu.get_barrier_semaphore()
    everyone = [to_voc(*o) for o in voc] + [to_dp(*o) for o in dps] + [pair, diag]
    for peer in everyone:
        pl.semaphore_signal(barrier, inc=1, device_id=peer, device_id_type=MESH)

    def slot_row(z, yy):
        return (z * 4 + lax.rem(yy + 2 * w, 4)) * SHARD

    def rows_of(z, yy, start=0, size=SHARD):
        at = pl.multiple_of(slot_row(z, yy) + start, 32)
        return h0.at[pl.ds(at, size)]

    load_emb = pltpu.make_async_copy(emb, ev, local_sem.at[0])
    load_emb.start()
    load_own = pltpu.make_async_copy(hid, rows_of(zh, y), local_sem.at[1])
    load_own.start()
    load_aux = pltpu.make_async_copy(aux, ar.at[zh * 4 + lax.rem(y + 2 * w, 4)], local_sem.at[2])
    load_aux.start()
    pl.semaphore_wait(barrier, len(everyone))

    sent = []

    def send(src, dst, s_sem, r_sem, peer, shared=False):
        copy = pltpu.make_async_remote_copy(
            src_ref=src, dst_ref=dst, send_sem=s_sem, recv_sem=r_sem,
            device_id=peer, device_id_type=MESH,
        )
        copy.start()
        if not shared:
            sent.append(copy)
        return copy

    zs = [zh, plus(zh, 3), plus(zh, 1), plus(zh, 2)]
    y1, y2 = [None] * 4, [None] * 4

    def y_first(j):
        z = zs[j]
        src = hid if j == 0 else rows_of(z, y)
        y1[j] = (
            send(src, rows_of(z, y), y_s.at[j, 0], y_r.at[j, 0], yp),
            send(src, rows_of(z, y), y_s.at[j, 1], y_r.at[j, 1], ym),
        )

    def y_second(j):
        z = zs[j]
        below, above = plus(y, 3), plus(y, 1)
        y1[j][0].wait_recv()
        one = rows_of(z, below, 0, 32)
        a = send(one, one, y_s.at[j, 2], y_r.at[j, 2], yp)
        y1[j][1].wait_recv()
        two = rows_of(z, above, 32, 32)
        b = send(two, two, y_s.at[j, 3], y_r.at[j, 3], ym)
        y2[j] = (a, b)

    sib_copies = [None] * 4

    def y_done(j):
        y2[j][0].wait_recv()
        y2[j][1].wait_recv()
        at = pl.ds(pl.multiple_of(zs[j] * CHUNK, CHUNK), CHUNK)
        sib_copies[j] = send(h0.at[at], h1.at[at], sib_s.at[j], sib_r.at[j], sib)

    own = rows_of(zh, y)
    z1p = send(hid, own, z_s.at[0], z_r.at[0], zp)
    z1m = send(hid, own, z_s.at[1], z_r.at[1], zm)
    y_first(0)
    load_aux.wait()
    mine = ar.at[zh * 4 + lax.rem(y + 2 * w, 4)]
    for oz, oy in voc:
        send(mine, mine, aux_s, aux_r, to_voc(oz, oy), True)
    load_own.wait()

    logit_copies = [None] * 4

    def logits_of(j):
        at = pl.ds(pl.multiple_of(zs[j] * CHUNK, CHUNK), CHUNK)

        @pl.loop(0, 2)
        def _(m):
            rows = pl.ds(pl.multiple_of(m * 512, 512), 512)
            both = lax.dot_general(
                ev[rows, :], h0[at, :], (((1,), (1,)), ((), ())), preferred_element_type=F32
            )
            lown[j, rows, :] = both[:, :HALF]
            lsend[j, rows, :] = both[:, HALF:]

        logit_copies[j] = send(lsend.at[j], lrecv.at[j], l_s.at[j], l_r.at[j], pair)

    def stats_of(j):
        logit_copies[j].wait_recv()

        def first(m, top):
            rows = pl.ds(pl.multiple_of(m * 256, 256), 256)
            both = lown[j, rows, :] + lrecv[j, rows, :]
            lown[j, rows, :] = both
            return jnp.maximum(top, jnp.max(both.reshape(32, 8, HALF), axis=0))

        top = lax.fori_loop(0, 4, first, jnp.full((8, HALF), -jnp.inf, F32))
        top = jnp.max(top, axis=0, keepdims=True)

        def second(m, total):
            rows = pl.ds(pl.multiple_of(m * 256, 256), 256)
            part_sum = jnp.exp(lown[j, rows, :] - top)
            return total + jnp.sum(part_sum.reshape(32, 8, HALF), axis=0)

        total = lax.fori_loop(0, 4, second, jnp.zeros((8, HALF), F32))
        st[zs[j]] = top
        st[zs[j] + 4] = jnp.sum(total, axis=0, keepdims=True)

    y_second(0)
    z1p.wait_recv()
    low = rows_of(plus(zh, 3), y, 0, 32)
    z2p = send(low, low, z_s.at[2], z_r.at[2], zp)
    y_first(1)
    z1m.wait_recv()
    high = rows_of(plus(zh, 1), y, 32, 32)
    z2m = send(high, high, z_s.at[3], z_r.at[3], zm)
    y_first(2)
    y_done(0)
    load_emb.wait()
    logits_of(0)
    z2p.wait_recv()
    z2m.wait_recv()
    y_first(3)
    y_second(1)
    y_second(2)
    y_done(1)
    logits_of(1)
    y_second(3)
    stats_of(0)
    y_done(2)
    logits_of(2)
    stats_of(1)
    y_done(3)
    logits_of(3)
    stats_of(2)
    stats_of(3)

    for k, (oz, oy) in enumerate(voc):
        send(st, sr.at[k], st_s, st_r, to_voc(oz, oy), True)
    pltpu.make_async_copy(ar.at[pl.ds(0, 15)], ar.at[pl.ds(0, 15)], aux_r).wait()
    pltpu.make_async_copy(sr, sr, st_r).wait()
    for zz in range(4):
        top = st[zz]
        for k in range(15):
            top = jnp.maximum(top, sr[k, zz])
        total = st[zz + 4] * jnp.exp(st[zz] - top)
        for k in range(15):
            total = total + sr[k, zz + 4] * jnp.exp(sr[k, zz] - top)
        rest = ar[zz * 4, 0:1, :] + ar[zz * 4 + 1, 0:1, :]
        big = jnp.maximum(top, rest)
        lse[zz] = big + jnp.log(total * jnp.exp(top - big) + jnp.exp(rest - big))

    d_copies = [None] * 4
    for j in range(4):
        z = zs[j]
        shift = lse[z]
        label = ar[z * 4, 1:2, :] + ar[z * 4 + 1, 1:2, :] - (v * ROWS).astype(F32)
        lane_row = lax.broadcasted_iota(jnp.int32, (BLK, HALF), 0).astype(F32)

        @pl.loop(0, 4)
        def _(xr):
            base = plus(x, xr) * 2 * BLK
            for core, dst in ((c, da), (1 - c, db)):
                row0 = pl.multiple_of(base + core * BLK, BLK)
                hit = (lane_row == label - row0.astype(F32)).astype(F32)
                dst[j, xr] = (jnp.exp(lown[j, pl.ds(row0, BLK), :] - shift) - hit).astype(BF16)

        d_copies[j] = (
            send(da.at[j], rpair.at[j], d_s.at[j, 0], d_r.at[j, 0], pair),
            send(db.at[j], rdiag.at[j], d_s.at[j, 1], d_r.at[j, 1], diag),
            send(db.at[j], rsib.at[j], d_s.at[j, 2], d_r.at[j, 2], sib),
        )

    def grad_piece(j, cols):
        at = pl.ds(pl.multiple_of(zs[j] * CHUNK, CHUNK), CHUNK)
        left = jnp.concatenate([da[j].reshape(512, HALF), rpair[j].reshape(512, HALF)], axis=1)
        right = jnp.concatenate([rsib[j].reshape(512, HALF), rdiag[j].reshape(512, HALF)], axis=1)
        both = jnp.dot(left, h0[at, cols], preferred_element_type=F32)
        both = both + jnp.dot(right, h1[at, cols], preferred_element_type=F32)
        both = both.reshape(4, BLK, NW)
        if j == 0:
            part[:, :, cols] = both
        else:
            part[:, :, cols] = part[:, :, cols] + both

    for j in range(3):
        for copy in d_copies[j]:
            copy.wait_recv()
        sib_copies[j].wait_recv()

        @pl.loop(0, NP)
        def _(n):
            grad_piece(j, pl.ds(pl.multiple_of(n * NW, 128), NW))

    for copy in d_copies[3]:
        copy.wait_recv()
    sib_copies[3].wait_recv()

    relay, whole = [None] * NP, [None] * NP

    def send_whole(n):
        cols = pl.ds(n * NW, NW)
        relay[n][0].wait_recv()
        part[1, 0:64, cols] = part[1, 0:64, cols] + ra[:, cols]
        one = send(part.at[1, :, cols], fa.at[:, cols], rs_s.at[n, 2], rs_r.at[n, 2], xp)
        relay[n][1].wait_recv()
        part[3, 64:128, cols] = part[3, 64:128, cols] + rb[:, cols]
        two = send(part.at[3, :, cols], fb.at[:, cols], rs_s.at[n, 3], rs_r.at[n, 3], xm)
        whole[n] = (one, two)

    for n in range(NP):
        cols = pl.ds(n * NW, NW)
        grad_piece(3, cols)
        relay[n] = (
            send(part.at[2, pl.ds(0, 64), cols], ra.at[:, cols], rs_s.at[n, 0], rs_r.at[n, 0], xp),
            send(part.at[2, pl.ds(64, 64), cols], rb.at[:, cols], rs_s.at[n, 1], rs_r.at[n, 1], xm),
        )
        if n > 0:
            send_whole(n - 1)
    send_whole(NP - 1)

    row_sum = jnp.zeros((BLK, 128), F32)
    vec[...] = jnp.zeros_like(vec)

    def slot(i):
        return i // PER, pl.ds(i % PER, 1)

    for t in range(TILES):
        if (t * 128) % NW == 0:
            for copy in whole[t * 128 // NW]:
                copy.wait_recv()
        cols = pl.ds(t * 128, 128)
        g = part[0, :, cols] + fa[:, cols] + fb[:, cols]
        part[0, :, cols] = g
        square = g * g + 1e-06
        row_sum = row_sum + square
        p, r = slot(t)
        vec[p, r, :] = jnp.sum(square, axis=0, keepdims=True)
    rowp[...] = row_sum
    row_copy = send(rowp, rowx, row_sem.at[0], row_sem.at[1], pair)
    state = jnp.transpose(jnp.broadcast_to(row_state[...], (BLK, 128)))
    row_copy.wait_recv()
    row_sq = jnp.sum(rowp[...] + rowx[...], axis=1, keepdims=True)
    new_rows = 0.9 * state + 0.1 * jnp.broadcast_to(row_sq, (BLK, 128)) / FULL
    nrows_out[...] = jnp.transpose(new_rows)[0:1, :]
    inverse = 1.0 / new_rows
    for t in range(TILES):
        g = part[0, :, pl.ds(t * 128, 128)]
        p, r = slot(TILES + t)
        vec[p, r, :] = jnp.sum(g * g * inverse, axis=0, keepdims=True)
    p, r = slot(2 * TILES)
    vec[p, r, :] = jnp.sum(new_rows, axis=0, keepdims=True)

    for k, (ox, oc) in enumerate(dps):
        piece = plus(x, ox) * 2 + lax.rem(c + oc, 2)
        send(vec.at[piece], vr.at[k], v_s, v_r, to_dp(ox, oc), True)
    pltpu.make_async_copy(vr, vr, v_r).wait()
    total = vec[d]
    for k in range(7):
        total = total + vr[k]
    ss[...] = total
    s2r[v] = total
    for oz, oy in voc:
        send(ss, s2r.at[v], s2_s, s2_r, to_voc(oz, oy), True)
    pltpu.make_async_copy(s2r.at[pl.ds(0, 15)], s2r.at[pl.ds(0, 15)], s2_r).wait()
    total = s2r[0]
    for k in range(1, 16):
        total = total + s2r[k]
    wv[d] = total
    for ox, oc in dps:
        send(wv.at[d], wv.at[d], w_s, w_r, to_dp(ox, oc), True)
    pltpu.make_async_copy(wv.at[pl.ds(0, 7)], wv.at[pl.ds(0, 7)], w_r).wait()

    p, r = slot(2 * TILES)
    mean = wv[p, r, :] / SLAB
    mean_out[...] = mean
    weighted = jnp.zeros((1, 128), F32)
    for t in range(TILES):
        cols = pl.ds(t * 128, 128)
        p, r = slot(t)
        new_cols = 0.9 * col_state[:, cols] + 0.1 * wv[p, r, :] / SLAB
        ncols_out[:, cols] = new_cols
        p, r = slot(TILES + t)
        weighted = weighted + wv[p, r, :] / new_cols
    weighted = jnp.sum(weighted, axis=1, keepdims=True) * mean
    qv[...] = jnp.broadcast_to(weighted, (8, 128))
    q_copy = send(qv, qx, q_sem.at[0], q_sem.at[1], pair)
    row_factor = lax.rsqrt(new_rows)
    q_copy.wait_recv()
    rms = jnp.sqrt((qv[0:1, :] + qx[0:1, :]) / (SLAB * FULL))
    clip = 1.0 / jnp.maximum(1.0, rms / 0.1)
    for t in range(TILES):
        cols = pl.ds(t * 128, 128)
        col_factor = lax.rsqrt(ncols_out[:, cols] / mean) * clip
        upd[:, cols] = part[0, :, cols] * row_factor * col_factor

    for copy in sent:
        copy.wait_send()
    pltpu.make_async_copy(ar.at[pl.ds(0, 15)], ar.at[pl.ds(0, 15)], aux_s).wait()
    pltpu.make_async_copy(sr, sr, st_s).wait()
    pltpu.make_async_copy(vr, vr, v_s).wait()
    pltpu.make_async_copy(s2r.at[pl.ds(0, 15)], s2r.at[pl.ds(0, 15)], s2_s).wait()
    pltpu.make_async_copy(wv.at[pl.ds(0, 7)], wv.at[pl.ds(0, 7)], w_s).wait()


def per_device(hidden, rest_lse, token_ids, slab_offset, embedding, row_state, col_state):
    odd = lax.rem(lax.axis_index("vocab_1"), 2)
    lines = jnp.stack([rest_lse.astype(F32), (token_ids - slab_offset[0]).astype(F32)])
    left = jnp.where(odd == 0, lines, 0.0)
    right = jnp.where(odd == 0, 0.0, lines)
    aux = jnp.pad(jnp.concatenate([left, right], axis=1), ((0, 6), (0, 0)))
    any_spec = pl.BlockSpec(memory_space=pl.ANY)
    vmem = pl.BlockSpec(memory_space=pltpu.VMEM)
    dma = pltpu.SemaphoreType.DMA
    V = pltpu.VMEM
    scratch = [
        V((ROWS, K), BF16), V((ROWS, K), BF16), V((ROWS, K), BF16),
        V((16, 8, 128), F32),
        V((4, ROWS, HALF), F32), V((4, ROWS, HALF), F32), V((4, ROWS, HALF), F32),
        V((8, 1, 128), F32), V((15, 8, 1, 128), F32), V((4, 1, 128), F32),
        V((4, 4, BLK, HALF), BF16), V((4, 4, BLK, HALF), BF16),
        V((4, 4, BLK, HALF), BF16), V((4, 4, BLK, HALF), BF16), V((4, 4, BLK, HALF), BF16),
        V((4, BLK, K), F32),
        V((64, K), F32), V((64, K), F32), V((BLK, K), F32), V((BLK, K), F32),
        V((BLK, 128), F32), V((BLK, 128), F32),
        V((8, 8, 128), F32), V((7, 8, 128), F32), V((8, 128), F32),
        V((16, 8, 128), F32), V((8, 8, 128), F32), V((8, 128), F32), V((8, 128), F32),
        dma((3,)), dma, dma, dma((4,)), dma((4,)), dma((4, 4)), dma((4, 4)),
        dma((4,)), dma((4,)), dma((4,)), dma((4,)), dma, dma, dma((4, 3)), dma((4, 3)),
        dma((NP, 4)), dma((NP, 4)), dma((2,)), dma, dma, dma, dma, dma, dma, dma((2,)),
    ]
    update, new_rows, new_cols, mean = pl.pallas_call(
        kernel,
        out_shape=(
            jax.ShapeDtypeStruct((BLK, K), F32),
            jax.ShapeDtypeStruct((1, BLK), F32),
            jax.ShapeDtypeStruct((1, K), F32),
            jax.ShapeDtypeStruct((1, 128), F32),
        ),
        in_specs=[any_spec, any_spec, any_spec, vmem, vmem],
        out_specs=(vmem, vmem, vmem, vmem),
        scratch_shapes=scratch,
        compiler_params=pltpu.CompilerParams(
            collective_id=0, has_side_effects=True, vmem_limit_bytes=62 * 1024 * 1024
        ),
    )(hidden, aux, embedding, row_state.reshape(1, BLK), col_state.reshape(1, K))
    return update, new_rows.reshape(BLK), new_cols.reshape(K), mean[0, :1]


def solution(mesh):
    finer = Mesh(
        mesh.devices.reshape(4, 2, 4, 4, mesh.shape["width"]),
        ("dp_0", "dp_1", "vocab_0", "vocab_1", "width"),
    )
    placed = (
        P(DP_VOCAB, "width"),
        P(DP_VOCAB),
        P(DP_VOCAB),
        P(),
        P(VOCAB, "width"),
        P(VOCAB_DP),
        P("width"),
    )
    return jax.shard_map(
        per_device,
        mesh=finer,
        in_specs=placed,
        out_specs=(P(VOCAB_DP, "width"), P(VOCAB_DP), P("width"), P()),
        check_vma=False,
    )
```

time: 409 us -> 200 us (0.49)
  waiting for transfers between devices: 194 us -> 0 us
  Pallas kernels: 0 us -> 187 us
  blocking collectives: 130 us -> 0 us
  starting transfers between devices: 28.9 us -> 0 us
  matrix products: 22.6 us -> 0 us
  between operations: 17.3 us -> 2.46 us
  other arithmetic: 11.3 us -> 3.33 us
    pallas_call x0 -> x1, Pallas kernels: none -> 187 us  [per_device(): pl.pallas_call(kernel, out_shape=(jax.ShapeDtypeStruct((BLK, K), F32), ja...]
    psum x9 -> x0, blocking collectives: 98.1 us -> none  [by_axis(): return functools.reduce(lax.psum, axes, shard)]
    all_gather x1 -> x0, waiting for transfers between devices: 75.4 us -> none  [in_one_piece(): whole = lax.all_gather(both, axis, axis=dim, tiled=True)]
    reduce_scatter x1 -> x0, waiting for transfers between devices: 61.3 us -> none  [per_device(): grad = lax.psum_scatter(full_grad, DP, scatter_dimension=0, tiled=True)]
    all_to_all x3 -> x0, waiting for transfers between devices: 56.9 us -> none  [the longest x1 48.5 us: sent_and_summed(): blocks = lax.all_to_all(split_up(shard, dim, peers), axis, 0, 0, tiled=True)]
    all_to_all x2 -> x0, blocking collectives: 32 us -> none  [sent_to_all(): lax.all_to_all(jnp.broadcast_to(shard[None], (peers, *shard.shape)), axis...]
    all_to_all x3 -> x0, starting transfers between devices: 28.8 us -> none  [the longest x2 18.5 us: sent_to_all(): lax.all_to_all(jnp.broadcast_to(shard[None], (peers, *shard.shape)), axis...]
    dot_general x2 -> x0, matrix products: 22.6 us -> none  [the longest x1 11.5 us: per_device(): lax.dot_general(dlogits, states, (((0,), (0,)), ((), ())), preferred_elem...]
  transfers between devices with their start and end apart: 5 -> 0, of which waited for: 4 -> 0; matrix products, arithmetic and copies ran while one was open for 3% -> 0% of each run, Pallas kernels for 0% -> 0%
where the time goes in v1:
time: 200 us; the launch traced here: 197 us
  Pallas kernels  187 us (94%)
  local copies, waits for them, and re-layouts  4.34 us (2%)
  other arithmetic  3.33 us (2%)
  between operations  2.46 us (1%)
    pallas_call x1, Pallas kernels, per_device(): pl.pallas_call(kernel, out_shape=(jax.ShapeDtypeStruct((BLK, K), F32), ja...  187 us

profile of v1, /device:TPU:10, one launch (start us, length us, event | category | flops | bytes accessed | tf_op | source)
XLA Modules:
  0.0 197.1 jit_solution(10139783098450030188)
XLA Ops:
  1.3 0.7 convert_bitcast_fusion
  1.9 0.7 bitcast_convert_fusion
  2.6 0.7 select_maximum_fusion.aux
  3.3 1.3 reshape.21.col_state
  4.6 187.0 %shard_map.102 = (f32[128,2688]{1,0:T(8,128)}, f32[1,128]{1,0:T(1,128)}, f32[1,2688]{1,0:T(1,128)}, f32[1,128]{1,0:T(1,128)}) custom-call(bf16[64,2688]{1,0:T(8,128)(2,1)} %hid.1, f32[8,128]{1,0:T(8,128)} %select_maximum_fusion.aux, bf16[1024,2688]{1,0:T(8,128)(2,1)} %emb.1, f32[1,128]{1,0:T(1,128)} %bitcast.11, f32[1,2688]{1,0:T(1,128)} %reshape.21.col_state), custom_call_target="tpu_custom_call" | custom-call | tf_op jit(solution)/shard_map/pallas_call | solution.py:399
  191.6 1.3 reduce
  192.9 0.0 copy-start.1
  192.9 0.0 copy-start
  192.9 2.5 %copy.15 = f32[128,2688]{1,0:T(8,128)} copy(f32[128,2688]{1,0:T(8,128)} %get-tuple-element.18) | data formatting | bytes 2752512
  195.4 0.0 copy-done.1
  195.4 0.5 copy.16
  195.9 0.0 copy-done
  (1 shorter events, 0.0 us)
Async XLA Ops:
  192.9 2.5 %copy-start.1 = (f32[1,128]{1,0:T(1,128)S(1)}, f32[1,128]{1,0:T(1,128)}, u32[]{:S(2)}) copy-start(f32[1,128]{1,0:T(1,128)} %get-tuple-element.9) | copy-start | bytes 1540
  192.9 3.0 %copy-start = (f32[1,128]{1,0:T(1,128)S(1)}, f32[1,128]{1,0:T(1,128)}, u32[]{:S(2)}) copy-start(f32[1,128]{1,0:T(1,128)} %get-tuple-element.11) | copy-start | bytes 1540

commit v2 on v1

--- a/solution.py
+++ b/solution.py
@@ -24,18 +24,17 @@
 TILES = K // 128
 SLAB = 16384
 FULL = 5376
-TOKENS_TOTAL_TILES = 43
 PER = 6
 NW = 896
 NP = K // NW
 
 
-def kernel(hid, aux, emb, row_state, col_state,
-           upd, nrows_out, ncols_out, mean_out,
-           h0, h1, ev, ar, lown, lsend, lrecv, st, sr, lse,
+def kernel(hid, emb, rest, ids, offset, row_state, col_state,
+           g_out, row_out, col_out, nrows_out, ncols_out, mean_out,
+           h0, h1, ev, lown, lsend, lrecv, sr, lse,
            da, db, rpair, rsib, rdiag, part, ra, rb, fa, fb,
            rowp, rowx, vec, vr, ss, s2r, wv, qv, qx,
-           local_sem, aux_s, aux_r, z_s, z_r, y_s, y_r, sib_s, sib_r, l_s, l_r,
+           local_sem, z_s, z_r, y_s, y_r, sib_s, sib_r, l_s, l_r,
            st_s, st_r, d_s, d_r, rs_s, rs_r, row_sem, v_s, v_r, s2_s, s2_r, w_s, w_r, q_sem):
     x = lax.axis_index("dp_0")
     c = lax.axis_index("dp_1")
@@ -65,7 +64,7 @@
     xp, xm = {"dp_0": plus(x, 1)}, {"dp_0": plus(x, 3)}
 
     barrier = pltpu.get_barrier_semaphore()
-    everyone = [to_voc(*o) for o in voc] + [to_dp(*o) for o in dps] + [pair, diag]
+    everyone = [zp, zm, yp, ym, xp, xm, sib, pair]
     for peer in everyone:
         pl.semaphore_signal(barrier, inc=1, device_id=peer, device_id_type=MESH)
 
@@ -80,8 +79,12 @@
     load_emb.start()
     load_own = pltpu.make_async_copy(hid, rows_of(zh, y), local_sem.at[1])
     load_own.start()
-    load_aux = pltpu.make_async_copy(aux, ar.at[zh * 4 + lax.rem(y + 2 * w, 4)], local_sem.at[2])
-    load_aux.start()
+    lane_odd = lax.broadcasted_iota(jnp.int32, (1, 128), 1) // 64
+    side = lane_odd == lax.rem(y, 2)
+    line = rest[...].astype(F32)
+    sr[0, 8] = jnp.where(side, jnp.concatenate([line, line], axis=1), 0.0)
+    line = (ids[...] - offset[0]).astype(F32)
+    sr[0, 9] = jnp.where(side, jnp.concatenate([line, line], axis=1), 0.0)
     pl.semaphore_wait(barrier, len(everyone))
 
     sent = []
@@ -130,10 +133,6 @@
     z1p = send(hid, own, z_s.at[0], z_r.at[0], zp)
     z1m = send(hid, own, z_s.at[1], z_r.at[1], zm)
     y_first(0)
-    load_aux.wait()
-    mine = ar.at[zh * 4 + lax.rem(y + 2 * w, 4)]
-    for oz, oy in voc:
-        send(mine, mine, aux_s, aux_r, to_voc(oz, oy), True)
     load_own.wait()
 
     logit_copies = [None] * 4
@@ -170,8 +169,8 @@
             return total + jnp.sum(part_sum.reshape(32, 8, HALF), axis=0)
 
         total = lax.fori_loop(0, 4, second, jnp.zeros((8, HALF), F32))
-        st[zs[j]] = top
-        st[zs[j] + 4] = jnp.sum(total, axis=0, keepdims=True)
+        sr[0, zs[j]] = top
+        sr[0, zs[j] + 4] = jnp.sum(total, axis=0, keepdims=True)
 
     y_second(0)
     z1p.wait_recv()
@@ -185,43 +184,49 @@
     y_done(0)
     load_emb.wait()
     logits_of(0)
+    y_second(1)
     z2p.wait_recv()
     z2m.wait_recv()
+    y_second(2)
     y_first(3)
-    y_second(1)
-    y_second(2)
     y_done(1)
     logits_of(1)
-    y_second(3)
     stats_of(0)
     y_done(2)
     logits_of(2)
+    y_second(3)
     stats_of(1)
     y_done(3)
     logits_of(3)
     stats_of(2)
     stats_of(3)
 
-    for k, (oz, oy) in enumerate(voc):
-        send(st, sr.at[k], st_s, st_r, to_voc(oz, oy), True)
-    pltpu.make_async_copy(ar.at[pl.ds(0, 15)], ar.at[pl.ds(0, 15)], aux_r).wait()
-    pltpu.make_async_copy(sr, sr, st_r).wait()
+    for oz, oy in voc:
+        send(sr.at[0], sr.at[oz * 4 + oy], st_s, st_r, to_voc(oz, oy), True)
+    pltpu.make_async_copy(sr.at[pl.ds(1, 15)], sr.at[pl.ds(1, 15)], st_r).wait()
+
+    def given(z, row):
+        from_z = lax.rem(zh + 4 - z, 4) * 4
+        one = from_z + lax.rem(y + 4 - 2 * w, 4)
+        two = from_z + lax.rem(y + 3 - 2 * w, 4)
+        return sr[one, row] + sr[two, row]
+
     for zz in range(4):
-        top = st[zz]
-        for k in range(15):
+        top = sr[0, zz]
+        for k in range(1, 16):
             top = jnp.maximum(top, sr[k, zz])
-        total = st[zz + 4] * jnp.exp(st[zz] - top)
-        for k in range(15):
+        total = sr[0, zz + 4] * jnp.exp(sr[0, zz] - top)
+        for k in range(1, 16):
             total = total + sr[k, zz + 4] * jnp.exp(sr[k, zz] - top)
-        rest = ar[zz * 4, 0:1, :] + ar[zz * 4 + 1, 0:1, :]
-        big = jnp.maximum(top, rest)
-        lse[zz] = big + jnp.log(total * jnp.exp(top - big) + jnp.exp(rest - big))
+        other = given(zz, 8)
+        big = jnp.maximum(top, other)
+        lse[zz] = big + jnp.log(total * jnp.exp(top - big) + jnp.exp(other - big))
 
     d_copies = [None] * 4
     for j in range(4):
         z = zs[j]
         shift = lse[z]
-        label = ar[z * 4, 1:2, :] + ar[z * 4 + 1, 1:2, :] - (v * ROWS).astype(F32)
+        label = given(z, 9) - (v * ROWS).astype(F32)
         lane_row = lax.broadcasted_iota(jnp.int32, (BLK, HALF), 0).astype(F32)
 
         @pl.loop(0, 4)
@@ -298,7 +303,7 @@
                 copy.wait_recv()
         cols = pl.ds(t * 128, 128)
         g = part[0, :, cols] + fa[:, cols] + fb[:, cols]
-        part[0, :, cols] = g
+        g_out[:, cols] = g
         square = g * g + 1e-06
         row_sum = row_sum + square
         p, r = slot(t)
@@ -310,9 +315,10 @@
     row_sq = jnp.sum(rowp[...] + rowx[...], axis=1, keepdims=True)
     new_rows = 0.9 * state + 0.1 * jnp.broadcast_to(row_sq, (BLK, 128)) / FULL
     nrows_out[...] = jnp.transpose(new_rows)[0:1, :]
+    row_out[...] = jnp.transpose(lax.rsqrt(new_rows))[0:1, :]
     inverse = 1.0 / new_rows
     for t in range(TILES):
-        g = part[0, :, pl.ds(t * 128, 128)]
+        g = g_out[:, pl.ds(t * 128, 128)]
         p, r = slot(TILES + t)
         vec[p, r, :] = jnp.sum(g * g * inverse, axis=0, keepdims=True)
     p, r = slot(2 * TILES)
@@ -343,48 +349,36 @@
     mean_out[...] = mean
     weighted = jnp.zeros((1, 128), F32)
     for t in range(TILES):
-        cols = pl.ds(t * 128, 128)
         p, r = slot(t)
-        new_cols = 0.9 * col_state[:, cols] + 0.1 * wv[p, r, :] / SLAB
-        ncols_out[:, cols] = new_cols
+        new_cols = 0.9 * col_state[t:t + 1, :] + 0.1 * wv[p, r, :] / SLAB
+        ncols_out[t:t + 1, :] = new_cols
         p, r = slot(TILES + t)
         weighted = weighted + wv[p, r, :] / new_cols
     weighted = jnp.sum(weighted, axis=1, keepdims=True) * mean
     qv[...] = jnp.broadcast_to(weighted, (8, 128))
     q_copy = send(qv, qx, q_sem.at[0], q_sem.at[1], pair)
-    row_factor = lax.rsqrt(new_rows)
     q_copy.wait_recv()
     rms = jnp.sqrt((qv[0:1, :] + qx[0:1, :]) / (SLAB * FULL))
     clip = 1.0 / jnp.maximum(1.0, rms / 0.1)
-    for t in range(TILES):
-        cols = pl.ds(t * 128, 128)
-        col_factor = lax.rsqrt(ncols_out[:, cols] / mean) * clip
-        upd[:, cols] = part[0, :, cols] * row_factor * col_factor
+    col_out[...] = lax.rsqrt(ncols_out[...] / mean) * clip
 
     for copy in sent:
         copy.wait_send()
-    pltpu.make_async_copy(ar.at[pl.ds(0, 15)], ar.at[pl.ds(0, 15)], aux_s).wait()
-    pltpu.make_async_copy(sr, sr, st_s).wait()
+    pltpu.make_async_copy(sr.at[pl.ds(1, 15)], sr.at[pl.ds(1, 15)], st_s).wait()
     pltpu.make_async_copy(vr, vr, v_s).wait()
     pltpu.make_async_copy(s2r.at[pl.ds(0, 15)], s2r.at[pl.ds(0, 15)], s2_s).wait()
     pltpu.make_async_copy(wv.at[pl.ds(0, 7)], wv.at[pl.ds(0, 7)], w_s).wait()
 
 
 def per_device(hidden, rest_lse, token_ids, slab_offset, embedding, row_state, col_state):
-    odd = lax.rem(lax.axis_index("vocab_1"), 2)
-    lines = jnp.stack([rest_lse.astype(F32), (token_ids - slab_offset[0]).astype(F32)])
-    left = jnp.where(odd == 0, lines, 0.0)
-    right = jnp.where(odd == 0, 0.0, lines)
-    aux = jnp.pad(jnp.concatenate([left, right], axis=1), ((0, 6), (0, 0)))
     any_spec = pl.BlockSpec(memory_space=pl.ANY)
     vmem = pl.BlockSpec(memory_space=pltpu.VMEM)
     dma = pltpu.SemaphoreType.DMA
     V = pltpu.VMEM
     scratch = [
         V((ROWS, K), BF16), V((ROWS, K), BF16), V((ROWS, K), BF16),
-        V((16, 8, 128), F32),
         V((4, ROWS, HALF), F32), V((4, ROWS, HALF), F32), V((4, ROWS, HALF), F32),
-        V((8, 1, 128), F32), V((15, 8, 1, 128), F32), V((4, 1, 128), F32),
+        V((16, 10, 1, 128), F32), V((4, 1, 128), F32),
         V((4, 4, BLK, HALF), BF16), V((4, 4, BLK, HALF), BF16),
         V((4, 4, BLK, HALF), BF16), V((4, 4, BLK, HALF), BF16), V((4, 4, BLK, HALF), BF16),
         V((4, BLK, K), F32),
@@ -392,25 +386,31 @@
         V((BLK, 128), F32), V((BLK, 128), F32),
         V((8, 8, 128), F32), V((7, 8, 128), F32), V((8, 128), F32),
         V((16, 8, 128), F32), V((8, 8, 128), F32), V((8, 128), F32), V((8, 128), F32),
-        dma((3,)), dma, dma, dma((4,)), dma((4,)), dma((4, 4)), dma((4, 4)),
+        dma((2,)), dma((4,)), dma((4,)), dma((4, 4)), dma((4, 4)),
         dma((4,)), dma((4,)), dma((4,)), dma((4,)), dma, dma, dma((4, 3)), dma((4, 3)),
         dma((NP, 4)), dma((NP, 4)), dma((2,)), dma, dma, dma, dma, dma, dma, dma((2,)),
     ]
-    update, new_rows, new_cols, mean = pl.pallas_call(
+    g, row_factor, col_factor, new_rows, new_cols, mean = pl.pallas_call(
         kernel,
         out_shape=(
             jax.ShapeDtypeStruct((BLK, K), F32),
             jax.ShapeDtypeStruct((1, BLK), F32),
-            jax.ShapeDtypeStruct((1, K), F32),
+            jax.ShapeDtypeStruct((TILES, 128), F32),
+            jax.ShapeDtypeStruct((1, BLK), F32),
+            jax.ShapeDtypeStruct((TILES, 128), F32),
             jax.ShapeDtypeStruct((1, 128), F32),
         ),
-        in_specs=[any_spec, any_spec, any_spec, vmem, vmem],
-        out_specs=(vmem, vmem, vmem, vmem),
+        in_specs=[any_spec, any_spec, vmem, vmem, pl.BlockSpec(memory_space=pltpu.SMEM), vmem, vmem],
+        out_specs=(vmem,) * 6,
         scratch_shapes=scratch,
         compiler_params=pltpu.CompilerParams(
             collective_id=0, has_side_effects=True, vmem_limit_bytes=62 * 1024 * 1024
         ),
-    )(hidden, aux, embedding, row_state.reshape(1, BLK), col_state.reshape(1, K))
+    )(
+        hidden, embedding, rest_lse.reshape(1, SHARD), token_ids.reshape(1, SHARD), slab_offset,
+        row_state.reshape(1, BLK), col_state.reshape(TILES, 128),
+    )
+    update = g * row_factor.reshape(BLK, 1) * col_factor.reshape(1, K)
     return update, new_rows.reshape(BLK), new_cols.reshape(K), mean[0, :1]
 
 

time: 200 us -> 185 us (0.925)
  Pallas kernels: 187 us -> 176 us
  local copies, waits for them, and re-layouts: 4.34 us -> 1.13 us
    pallas_call x1, Pallas kernels: 187 us -> 176 us  [per_device(): pl.pallas_call(kernel, out_shape=(jax.ShapeDtypeStruct((BLK, K), F32), ja...]
    mul x0 -> x1, other arithmetic: none -> 2.62 us  [per_device(): update = g * row_factor.reshape(BLK, 1) * col_factor.reshape(1, K)]
where the time goes in v2:
time: 185 us; the launch traced here: 182 us
  Pallas kernels  176 us (95%)
  other arithmetic  2.62 us (1%)
  between operations  2.48 us (1%)
    pallas_call x1, Pallas kernels, per_device(): pl.pallas_call(kernel, out_shape=(jax.ShapeDtypeStruct((BLK, K), F32), ja...  176 us

profile of v2, /device:TPU:10, one launch (start us, length us, event | category | flops | bytes accessed | tf_op | source)
XLA Modules:
  0.0 181.7 jit_solution(11732610482017582105)
XLA Ops:
  1.3 175.5 %shard_map.102 = (f32[128,2688]{1,0:T(8,128)}, f32[1,128]{1,0:T(1,128)}, f32[21,128]{1,0:T(8,128)}, f32[1,128]{1,0:T(1,128)}, f32[21,128]{1,0:T(8,128)}, /*index=5*/f32[1,128]{1,0:T(1,128)}) custom-call(bf16[64,2688]{1,0:T(8,128)(2,1)} %hid.1, bf16[1024,2688]{1,0:T(8,128)(2,1)} %emb.1, bf16[1,64]{1,0:T(2,128)(2,1)} %bitcast.13, s32[1,64]{1,0:T(1,128)} %bitcast.14, ...), custom_call_target="tpu_custom_call" | custom-call | tf_op jit(solution)/shard_map/pallas_call | solution.py:393
  176.8 0.0 copy-start.2
  176.8 0.0 copy-start
  176.8 0.0 copy-start.1
  176.8 2.6 %multiply_multiply_fusion = f32[128,2688]{1,0:T(8,128)} fusion(f32[128,2688]{1,0:T(8,128)} %get-tuple-element.10, f32[2688]{0:T(1024)} %bitcast.11, f32[128]{0:T(128)} %bitcast.16), kind=kLoop, calls=%fused_computation | loop fusion | flops 688128 | bytes 2763776 | tf_op jit(solution)/shard_map/mul | solution.py:413
  179.4 0.0 copy-done.2
  179.4 0.5 copy.15
  180.0 0.0 copy-done
  180.0 0.6 copy.16
  180.6 0.0 copy-done.1
Async XLA Ops:
  176.8 2.6 %copy-start.2 = (f32[1,128]{1,0:T(1,128)S(1)}, f32[1,128]{1,0:T(1,128)}, u32[]{:S(2)}) copy-start(f32[1,128]{1,0:T(1,128)} %get-tuple-element.13) | copy-start | bytes 1540
  176.8 3.2 %copy-start = (f32[21,128]{1,0:T(8,128)S(1)}, f32[21,128]{1,0:T(8,128)}, u32[]{:S(2)}) copy-start(f32[21,128]{1,0:T(8,128)} %get-tuple-element.14) | copy-start | bytes 32260
  176.8 3.7 %copy-start.1 = (f32[1,128]{1,0:T(1,128)S(1)}, f32[1,128]{1,0:T(1,128)}, u32[]{:S(2)}) copy-start(f32[1,128]{1,0:T(1,128)} %get-tuple-element.15) | copy-start | bytes 1540
